TPU v7x, 1024 devices: a whole 4x8x16 slice. The times are simulated.
1024 devices in a mesh: zero: 8 (over x, core), expert: 128 (over y, z).
Axes of the slice: x: 4, y: 8, z: 16, core: 2. Of those that a mesh axis runs over, the one named last changes fastest.
Arguments:
- mom_values: bfloat16 [512, 512, 2048], P('expert', 'zero'), may hold values from -1 to 1
- mom_scale: float32 [512, 512], P('expert', 'zero'), may hold values from 0.5 to 2
- gradients: bfloat16 [512, 512, 2048], P('expert', 'zero'), may hold values from -32400 to 32400
Outputs:
- update: bfloat16 [512, 512, 2048], P('expert', 'zero')
All inputs are finite; a program needn't handle non-finite values.
Results may differ from a plain program's by a relative error of at most 0.0061.
Values may be sent and summed in bfloat16 or wider, within the bound.
A program may use at most 32 MiB of HBM per device.

v0:
```python
import jax
import jax.numpy as jnp
from jax import lax
from jax.sharding import Mesh
from jax.sharding import PartitionSpec as P

MODEL_D = 2048
ZERO_EXPERT = ("zero_0", "zero_1", "expert_0", "expert_1")
ZERO = ("zero_0", "zero_1")
EXPERT = ("expert_0", "expert_1")


coeff_linear = 3.4445
coeff_cubic = -4.775
coeff_quintic = 2.0315
decay_rate = 0.95
clip_level = 1.0
epsilon = 1e-06


def one_axis_at_a_time(array, axes):
    for axis in axes:
        array = lax.psum(array, axis)
    return array


def swapped(array, axis, apart):
    return lax.ppermute(array, axis, [(i, i ^ 1 << apart) for i in range(lax.axis_size(axis))])


def newton_chain(gram_matrix, squared_norm):
    identity = jnp.eye(gram_matrix.shape[0], dtype=jnp.float32)
    gnorm = (gram_matrix / (squared_norm + epsilon)).astype(jnp.bfloat16)
    square = jnp.dot(gnorm, gnorm, preferred_element_type=jnp.float32)
    polynomial = (
        coeff_linear * identity + coeff_cubic * gnorm.astype(jnp.float32) + coeff_quintic * square
    ).astype(jnp.bfloat16)
    halfway = jnp.dot(polynomial, gnorm, preferred_element_type=jnp.float32).astype(jnp.bfloat16)
    conjugated = jnp.dot(halfway, polynomial.T, preferred_element_type=jnp.float32).astype(
        jnp.bfloat16
    )
    square = jnp.dot(conjugated, conjugated, preferred_element_type=jnp.float32)
    quintic = (coeff_cubic * conjugated.astype(jnp.float32) + coeff_quintic * square).astype(
        jnp.bfloat16
    )
    product = jnp.dot(quintic, polynomial, preferred_element_type=jnp.float32)
    polynomial = (coeff_linear * polynomial.astype(jnp.float32) + product).astype(jnp.bfloat16)
    return polynomial


def final_update(polynomial, matrix, squared_norm):
    applied = jnp.dot(polynomial, matrix, preferred_element_type=jnp.float32)
    return (applied * (jnp.sqrt(jnp.float32(MODEL_D)) / jnp.sqrt(squared_norm + epsilon))).astype(
        jnp.bfloat16
    )


def per_device(mom_values, mom_scale, gradients):
    local_sum = jnp.sum(jnp.square(gradients.astype(jnp.float32)))
    summed = one_axis_at_a_time(local_sum, ZERO_EXPERT)
    entries = gradients.size * lax.axis_size(ZERO) * lax.axis_size(EXPERT)
    clip_factor = clip_level / jnp.sqrt(summed / entries + epsilon)
    momentum = mom_values.astype(jnp.float32) * mom_scale[:, :, None]
    new_mom = (decay_rate * momentum + clip_factor * gradients.astype(jnp.float32)).astype(
        jnp.bfloat16
    )
    groups = lax.axis_size(ZERO)
    slot_count, shard_rows, full_width = new_mom.shape
    half_width = full_width // 2
    outgoing = jnp.concatenate([new_mom[:, :, :half_width], new_mom[:, :, half_width:]], 0)
    columns = lax.all_to_all(outgoing, ZERO, split_axis=0, concat_axis=0, tiled=True).reshape(
        groups * shard_rows, half_width
    )
    partial_value = jnp.dot(columns, columns.T, preferred_element_type=jnp.float32)
    partner_bit = groups.bit_length() - 2
    gram_matrix = partial_value + swapped(
        partial_value.astype(jnp.bfloat16), ZERO, partner_bit
    ).astype(partial_value.dtype)
    squared_norm = jnp.trace(gram_matrix)
    polynomial = newton_chain(gram_matrix, squared_norm)
    result = final_update(polynomial, columns, squared_norm).reshape(groups, shard_rows, half_width)
    returned = lax.all_to_all(result, ZERO, split_axis=0, concat_axis=0, tiled=True)
    return jnp.concatenate([returned[:slot_count], returned[slot_count:]], 2)


def solution(mesh):
    finer = Mesh(mesh.devices.reshape(4, 2, 8, 16), ("zero_0", "zero_1", "expert_0", "expert_1"))
    return jax.shard_map(
        per_device,
        mesh=finer,
        in_specs=(P(EXPERT, ZERO, None), P(EXPERT, ZERO), P(EXPERT, ZERO, None)),
        out_specs=P(EXPERT, ZERO, None),
        check_vma=False,
    )
```

profile of v0, /device:TPU:1, one launch (start us, length us, event | category | flops | bytes accessed | tf_op | source)
XLA Modules:
  0.0 142.7 jit_solution(120607408937986217)
XLA Ops:
  0.0 0.0 copy-start
  0.0 0.0 copy-start.1
  0.0 2.5 %fusion = f32[]{:T(128)} fusion(bf16[4,64,2048]{2,1,0:T(8,128)(2,1)} %param.5), kind=kLoop, calls=%fused_computation.2 | loop fusion | flops 1572863 | bytes 1048580 | tf_op jit(solution)/shard_map/reduce_sum | solution.py:59
  2.5 9.9 %psum.28 = f32[]{:T(128)} all-reduce(f32[]{:T(128)} %fusion), channel_id=1, replica_groups=mesh['zero_0'=4,'zero_1'=2,'expert_0'=8,'expert_1'=16] {'zero_0'}, use_global_device_ids=true, to_apply=%region_1.0 | all-reduce | flops 1 | bytes 8 | tf_op jit(solution)/shard_map/psum | solution.py:23
  12.4 15.3 %psum.29 = f32[]{:T(128)} all-reduce(f32[]{:T(128)} %psum.28), channel_id=1, replica_groups=mesh['zero_0'=4,'zero_1'=2,'expert_0'=8,'expert_1'=16] {'zero_1'}, use_global_device_ids=true, to_apply=%region_2.0 | all-reduce | flops 1 | bytes 8 | tf_op jit(solution)/shard_map/psum | solution.py:23
  27.7 11.4 %psum.30 = f32[]{:T(128)} all-reduce(f32[]{:T(128)} %psum.29), channel_id=1, replica_groups=mesh['zero_0'=4,'zero_1'=2,'expert_0'=8,'expert_1'=16] {'expert_0'}, use_global_device_ids=true, to_apply=%region_3.0 | all-reduce | flops 1 | bytes 8 | tf_op jit(solution)/shard_map/psum | solution.py:23
  39.0 30.2 %psum.31 = f32[]{:T(128)} all-reduce(f32[]{:T(128)} %psum.30), channel_id=1, replica_groups=mesh['zero_0'=4,'zero_1'=2,'expert_0'=8,'expert_1'=16] {'expert_1'}, use_global_device_ids=true, to_apply=%region_4.0 | all-reduce | flops 1 | bytes 8 | tf_op jit(solution)/shard_map/psum | solution.py:23
  69.9 0.0 copy-done
  69.9 0.0 copy-done.1
  70.0 1.7 %fusion.2 = bf16[4,64,2048]{2,1,0:T(8,128)(2,1)S(1)} fusion(bf16[4,64,2048]{2,1,0:T(8,128)(2,1)S(1)} %copy-done, bf16[4,64,2048]{2,1,0:T(8,128)(2,1)} %param.3, f32[]{:T(128)S(6)} %sqrt.6, f32[4,64]{1,0:T(4,128)S(1)} %copy-done.1), kind=kLoop, calls=%fused_computation.4 | loop fusion | flops 3670016 | bytes 3146756 | tf_op jit(solution)/shard_map/convert_element_type | solution.py:64
  71.7 0.1 fusion.13
  71.8 0.1 pad_maximum_fusion
  71.9 28.4 %all_to_all.10 = bf16[8,64,1024]{2,1,0:T(8,128)(2,1)S(1)} all-to-all(bf16[8,64,1024]{2,1,0:T(8,128)(2,1)S(1)} %pad_maximum_fusion), channel_id=1, replica_groups=mesh['zero_0'=4,'zero_1'=2,'expert_0'=8,'expert_1'=16] {'zero_0','zero_1'}, dimensions={0} | all-to-all | bytes 2097152 | tf_op jit(solution)/shard_map/all_to_all | solution.py:71
  100.3 0.7 fusion.14
  101.1 2.5 %collective-permute-start = (bf16[512,512]{1,0:T(8,128)(2,1)S(1)}, bf16[512,512]{1,0:T(8,128)(2,1)S(1)}, u32[]{:S(2)}, u32[]{:S(2)}) collective-permute-start(bf16[512,512]{1,0:T(8,128)(2,1)S(1)} %get-tuple-element.9), channel_id=1, source_target_pairs={{0,512},{128,640},{256,768},{384,896},{512,0},{640,128},{768,256},... | collective-permute-start | bytes 1572872 | tf_op jit(solution)/shard_map/ppermute | solution.py:28
  103.6 13.3 %collective-permute-done = bf16[512,512]{1,0:T(8,128)(2,1)S(1)} collective-permute-done((bf16[512,512]{1,0:T(8,128)(2,1)S(1)}, bf16[512,512]{1,0:T(8,128)(2,1)S(1)}, u32[]{:S(2)}, u32[]{:S(2)}) %collective-permute-start) | collective-permute-done | bytes 524320 | tf_op jit(solution)/shard_map/ppermute | solution.py:28
  116.9 0.7 select_reduce_fusion
  118.3 0.2 divide_convert_fusion
  118.4 0.4 fusion.5
  118.9 0.0 copy-start.2
  118.9 0.7 convolution_convert_fusion
  119.6 0.1 copy-done.2
  119.7 0.4 fusion.6
  120.1 2.2 %multiply_convert_fusion = bf16[512,1024]{1,0:T(8,128)(2,1)S(1)} fusion(bf16[512,1024]{1,0:T(8,128)(2,1)S(1)} %bitcast.15, bf16[512,512]{1,0:T(8,128)(2,1)S(1)} %fusion.6, bf16[512,512]{1,0:T(8,128)(2,1)} %copy-done.2, f32[]{:T(128)S(6)} %div.16), kind=kOutput, calls=%fused_computation.5 | convolution fusion | flops 807403520 | bytes 3145732 | tf_op jit(solution)/shard_map/dot_general | solution.py:52
  122.3 19.2 %all_to_all.11 = bf16[8,64,1024]{2,1,0:T(8,128)(2,1)S(1)} all-to-all(bf16[8,64,1024]{2,1,0:T(8,128)(2,1)S(1)} %bitcast.16), channel_id=1, replica_groups=mesh['zero_0'=4,'zero_1'=2,'expert_0'=8,'expert_1'=16] {'zero_0','zero_1'}, dimensions={0} | all-to-all | bytes 2097152 | tf_op jit(solution)/shard_map/all_to_all | solution.py:82
  141.6 0.1 fusion.12
  141.7 1.1 pad_maximum_fusion.1
Async XLA Ops:
  0.0 69.9 %copy-start = (bf16[4,64,2048]{2,1,0:T(8,128)(2,1)S(1)}, bf16[4,64,2048]{2,1,0:T(8,128)(2,1)}, u32[]{:S(2)}) copy-start(bf16[4,64,2048]{2,1,0:T(8,128)(2,1)} %param.5) | copy-start | bytes 3145732
  0.0 69.9 %copy-start.1 = (f32[4,64]{1,0:T(4,128)S(1)}, f32[4,64]{1,0:T(4,128)}, u32[]{:S(2)}) copy-start(f32[4,64]{1,0:T(4,128)} %param.4) | copy-start | bytes 3076
  101.1 15.8 %collective-permute-start = (bf16[512,512]{1,0:T(8,128)(2,1)S(1)}, bf16[512,512]{1,0:T(8,128)(2,1)S(1)}, u32[]{:S(2)}, u32[]{:S(2)}) collective-permute-start(bf16[512,512]{1,0:T(8,128)(2,1)S(1)} %get-tuple-element.9), channel_id=1, source_target_pairs={{0,512},{128,640},{256,768},{384,896},{512,0},{640,128},{768,256},... | collective-permute-start | bytes 1572872 | tf_op jit(solution)/shard_map/ppermute | solution.py:28
  118.9 0.8 copy-start.2
where the time goes:
time: 143 us
  blocking collectives  114 us (80%)
  waiting for transfers between devices  13.3 us (9%)
  other arithmetic  6.19 us (4%)
  matrix products  4.52 us (3%)
  starting transfers between devices  2.51 us (2%)
  between operations  1.5 us (1%)
    psum x4, blocking collectives, one_axis_at_a_time(): array = lax.psum(array, axis)  66.8 us
    all_to_all x1, blocking collectives, per_device(): lax.all_to_all(outgoing, ZERO, split_axis=0, concat_axis=0, tiled=True)  28.4 us
    all_to_all x1, blocking collectives, per_device(): lax.all_to_all(result, ZERO, split_axis=0, concat_axis=0, tiled=True)  19.2 us
    ppermute x1, waiting for transfers between devices, swapped(): lax.ppermute(array, axis, [(i, i ^ 1 << apart) for i in range(lax.axis_si...  13.3 us
  transfers between devices with their start and end apart: 1, of which 1 were waited for; matrix products, arithmetic and copies ran while one was open for 0% of the time, Pallas kernels for 0%

commit v1 on v0

v1 whole, which is shorter than its diff:
```python
import jax
import jax.numpy as jnp
from jax import lax
from jax.experimental import pallas as pl
from jax.experimental.pallas import tpu as pltpu
from jax.sharding import Mesh
from jax.sharding import PartitionSpec as P

AXES = ("x", "core", "y", "z")
ZERO = ("x", "core")
EXPERT = ("y", "z")

coeff_linear = 3.4445
coeff_cubic = -4.775
coeff_quintic = 2.0315
decay_rate = 0.95
epsilon = 1e-06

WIDTH = 256
RAW = 1
REACH = 4

F32, BF16 = jnp.float32, jnp.bfloat16


def remote(src, dst, send_sem, recv_sem, **where):
    return pltpu.make_async_remote_copy(
        src_ref=src,
        dst_ref=dst,
        send_sem=send_sem,
        recv_sem=recv_sem,
        device_id=where,
        device_id_type=pl.DeviceIdType.MESH,
    )


def arrived(dst, recv_sem, send_sem, **where):
    remote(dst, dst, send_sem, recv_sem, **where).wait_recv()


def dot(a, b):
    return jnp.dot(a, b, preferred_element_type=F32)


def dot_t(a, b):
    return lax.dot_general(a, b, (((1,), (1,)), ((), ())), preferred_element_type=F32)


def near_offsets(n):
    if n <= 2 * REACH:
        return list(range(1, n))
    assert n == 4 * REACH
    return [o * s for o in range(REACH, 0, -1) for s in (1, -1)]


def kernel(
    entries, sizes,
    mv, ms, gr, out,
    gbuf, mbuf, xs_out, xs_in, ys_out, ys_in, zs_out, zs_in, far_out, far_in,
    ms_in, own_sc, src_sc, hop, d2, d1, xc, fresh, fresh_p, gram, g_out, g_in,
    n_ref, p_ref, c_ref, ubuf, uhop,
    loc_s, xs_s, ys_s, zs_s, far_s, ms_s, hop_s, d2_s, d1_s, f_s, fp_s, g_s, o_hop, o_d2, o_d1, o_p, o_own,
):
    ny, nz = sizes
    rows, half = gbuf.shape[2], gbuf.shape[3]
    chunks = half // WIDTH
    ff = 8 * rows
    x, c, y, z = (lax.axis_index(a) for a in AXES)
    xp, xm, x2 = lax.rem(x + 1, 4), lax.rem(x + 3, 4), lax.rem(x + 2, 4)
    other = 1 - c
    sides = (xp, xm)
    y_near, z_near = near_offsets(ny), near_offsets(nz)
    at_y = [lax.rem(y + (o + ny), ny) for o in y_near]
    at_z = [lax.rem(z + (o + nz), nz) for o in z_near]
    group = [(dx, dc) for dx in (2, 1, 3, 0) for dc in (0, 1) if dx or dc]

    def member(dx, dc):
        return {"x": lax.rem(x + dx, 4), "core": other if dc else c}

    barrier = pltpu.get_barrier_semaphore()
    for t in at_z:
        pl.semaphore_signal(barrier, inc=1, device_id={"z": t}, device_id_type=pl.DeviceIdType.MESH)
    for t in at_y:
        pl.semaphore_signal(barrier, inc=1, device_id={"y": t}, device_id_type=pl.DeviceIdType.MESH)
    for dx, dc in group:
        pl.semaphore_signal(barrier, inc=1, device_id=member(dx, dc), device_id_type=pl.DeviceIdType.MESH)

    local = [
        pltpu.make_async_copy(src.at[:, :, pl.ds(h * half, half)], dst.at[h], loc_s.at[t, h])
        for t, (src, dst) in enumerate(((gr, gbuf), (mv, mbuf)))
        for h in range(2)
    ]
    for copy in local:
        copy.start()

    acc = None
    for h in range(2):
        local[h].wait()
        for m in range(4):
            g = gbuf[h, m].astype(F32)
            part = jnp.sum((g * g).reshape(rows // 8, 8, half), axis=0)
            acc = part if acc is None else acc + part
    lanes = acc[:, :128]
    for i in range(1, half // 128):
        lanes = lanes + acc[:, i * 128 : (i + 1) * 128]
    xs_out[...] = jnp.sum(lanes, axis=0, keepdims=True)

    ii = lax.broadcasted_iota(jnp.int32, (rows, rows), 0)
    jj = lax.broadcasted_iota(jnp.int32, (rows, rows), 1)
    mat = lax.broadcasted_iota(jnp.int32, (4, rows), 0)

    def column(values, m):
        row = jnp.sum(jnp.where(mat == m, values, 0.0), axis=0, keepdims=True)
        col = jnp.sum(jnp.where(ii == jj, row, 0.0), axis=1, keepdims=True)
        return jnp.broadcast_to(decay_rate * col, (rows, WIDTH))

    own = ms[...]
    for i, m in enumerate((xp, xm, x)):
        own_sc[i] = column(own, m)

    pl.semaphore_wait(barrier, len(at_y) + len(at_z) + len(group))
    sent = []

    def send(*args, **where):
        copy = remote(*args, **where)
        copy.start()
        sent.append(copy)

    for dx, dc in group:
        i = 2 * dx + dc
        send(xs_out, xs_in.at[i], xs_s.at[0, i], xs_s.at[1, i], **member(dx, dc))
    for s, to in enumerate((xp, xm, x2)):
        for k in range(2):
            send(ms, ms_in.at[s, c], ms_s.at[0, s, k], ms_s.at[1, s, c], x=to, core=k)
    for t, src in enumerate((gr, mv)):
        for d in range(2):
            send(
                src.at[x2, :, pl.ds(d * half, half)], hop.at[t, d],
                hop_s.at[0, t, d], hop_s.at[1, t, d], x=sides[d], core=c,
            )
    if RAW:
        for t, src in enumerate((gr, mv)):
            for d in range(2):
                for k in range(2):
                    send(
                        src.at[sides[d], :, pl.ds(k * half, RAW * WIDTH)], d1.at[t, d, c],
                        d1_s.at[0, t, d, k], d1_s.at[1, t, d, c], x=sides[d], core=k,
                    )

    def forward(t):
        for d in range(2):
            arrived(hop.at[t, d], hop_s.at[1, t, d], hop_s.at[0, t, d], x=sides[d], core=c)
            send(hop.at[t, d], d2.at[t, c], d2_s.at[0, t, d], d2_s.at[1, t, c], x=sides[d], core=d)

    total = xs_out[...]
    for dx, dc in group:
        i = 2 * dx + dc
        arrived(xs_in.at[i], xs_s.at[1, i], xs_s.at[0, i], **member(dx, dc))
        total = total + xs_in[i]
    if y_near:
        ys_out[...] = total
        for i, t in enumerate(at_y):
            send(ys_out, ys_in.at[i], ys_s.at[0, i], ys_s.at[1, i], y=t)
    for s, to in enumerate((xp, xm, x2)):
        for k in range(2):
            arrived(ms_in.at[s, k], ms_s.at[1, s, k], ms_s.at[0, s, k], x=to, core=k)
            src_sc[s, k] = column(ms_in[s, k], x)
    forward(0)
    for i, t in enumerate(at_y):
        arrived(ys_in.at[i], ys_s.at[1, i], ys_s.at[0, i], y=t)
        total = total + ys_in[i]
    if z_near:
        zs_out[...] = total
        for i, t in enumerate(at_z):
            send(zs_out, zs_in.at[i], zs_s.at[0, i], zs_s.at[1, i], z=t)
    forward(1)
    ahead = behind = None
    for i, (o, t) in enumerate(zip(z_near, at_z)):
        arrived(zs_in.at[i], zs_s.at[1, i], zs_s.at[0, i], z=t)
        total = total + zs_in[i]
        if o < 0:
            ahead = zs_in[i] if ahead is None else ahead + zs_in[i]
        elif o < REACH:
            behind = zs_in[i] if behind is None else behind + zs_in[i]
    if nz > 2 * REACH:
        far_out[0] = ahead
        far_out[1] = behind
        for i, t in ((0, lax.rem(z + nz - REACH, nz)), (1, lax.rem(z + REACH, nz))):
            send(far_out.at[i], far_in.at[i], far_s.at[0, i], far_s.at[1, i], z=t)
        for i, t in ((0, lax.rem(z + REACH, nz)), (1, lax.rem(z + nz - REACH, nz))):
            arrived(far_in.at[i], far_s.at[1, i], far_s.at[0, i], z=t)
            total = total + far_in[i]
    clip = lax.rsqrt(jnp.sum(total, axis=1, keepdims=True) / entries + epsilon)

    def momentum(values, scale, gradient):
        return (values.astype(F32) * scale + clip * gradient.astype(F32)).astype(BF16)

    def cols(k):
        return pl.ds(k * WIDTH, WIDTH)

    for copy in local[2:]:
        copy.wait()
    my_rows = pl.ds(pl.multiple_of((2 * x + c) * rows, rows), rows)
    for k in range(RAW, chunks):
        for d in range(2):
            for h in range(2):
                fresh[k - RAW, d, h] = momentum(
                    mbuf[h, sides[d], :, cols(k)], own_sc[d], gbuf[h, sides[d], :, cols(k)]
                )
                send(
                    fresh.at[k - RAW, d, h], xc.at[k, my_rows],
                    f_s.at[0, k, d, h], f_s.at[1, k, d, c], x=sides[d], core=h,
                )
    for k in range(chunks):
        fresh_p[k] = momentum(mbuf[other, x, :, cols(k)], own_sc[2], gbuf[other, x, :, cols(k)])
    send(fresh_p, xc.at[:, my_rows], fp_s.at[0], fp_s.at[1], x=x, core=other)
    for k in range(chunks):
        xc[k, my_rows] = momentum(mbuf[c, x, :, cols(k)], own_sc[2], gbuf[c, x, :, cols(k)])

    def rows_of(chip, core):
        return pl.ds(pl.multiple_of((2 * chip + core) * rows, rows), rows)

    came = (xm, xp)
    for d in range(2):
        for k in range(2):
            if RAW:
                for t in range(2):
                    arrived(d1.at[t, d, k], d1_s.at[1, t, d, k], d1_s.at[0, t, d, k], x=sides[d], core=k)
                for i in range(RAW):
                    xc[i, rows_of(came[d], k)] = momentum(
                        d1[1, d, k, :, cols(i)], src_sc[d, k], d1[0, d, k, :, cols(i)]
                    )
    for k in range(2):
        for t in range(2):
            arrived(d2.at[t, k], d2_s.at[1, t, k], d2_s.at[0, t, k], x=xp, core=k)
        for i in range(chunks):
            xc[i, rows_of(x2, k)] = momentum(d2[1, k, :, cols(i)], src_sc[2, k], d2[0, k, :, cols(i)])
    arrived(xc.at[:, rows_of(x, other)], fp_s.at[1], fp_s.at[0], x=x, core=other)

    tall = ff // 2
    for k in range(chunks):
        if k >= RAW:
            for d in range(2):
                for h in range(2):
                    arrived(
                        xc.at[k, rows_of(came[d], h)], f_s.at[1, k, d, h], f_s.at[0, k, d, h],
                        x=sides[d], core=h,
                    )
        for r in range(2):
            part = dot_t(xc[k, pl.ds(r * tall, tall)], xc[k])
            if k:
                part = gram[pl.ds(r * tall, tall)] + part
            gram[pl.ds(r * tall, tall)] = part
            if k == chunks - 1:
                g_out[r] = part.astype(BF16)
                send(g_out.at[r], g_in.at[r], g_s.at[0, r], g_s.at[1, r], x=x, core=other)
    norm = None
    diag = lax.broadcasted_iota(jnp.int32, (128, 128), 0) == lax.broadcasted_iota(jnp.int32, (128, 128), 1)
    for r in range(2):
        arrived(g_in.at[r], g_s.at[1, r], g_s.at[0, r], x=x, core=other)
        whole = gram[pl.ds(r * tall, tall)] + g_in[r].astype(F32)
        gram[pl.ds(r * tall, tall)] = whole
        for b in range(tall // 128):
            square = whole[b * 128 : (b + 1) * 128, r * tall + b * 128 : r * tall + (b + 1) * 128]
            masked = jnp.where(diag, square, 0.0)
            norm = masked if norm is None else norm + masked
    norm = jnp.sum(jnp.sum(norm, axis=0, keepdims=True), axis=1, keepdims=True) + epsilon
    inverse = 1.0 / norm
    scale = (2.0 * half) ** 0.5 * lax.rsqrt(norm)

    for r in range(2):
        at = pl.ds(r * tall, tall)
        n_ref[at] = (gram[at] * inverse).astype(BF16)
    for r in range(2):
        at = pl.ds(r * tall, tall)
        eye = lax.broadcasted_iota(jnp.int32, (tall, ff), 0) + r * tall == lax.broadcasted_iota(jnp.int32, (tall, ff), 1)
        square = dot(n_ref[at], n_ref[...])
        p_ref[at] = (
            jnp.where(eye, coeff_linear, 0.0) + coeff_cubic * n_ref[at].astype(F32) + coeff_quintic * square
        ).astype(BF16)
    for r in range(2):
        at = pl.ds(r * tall, tall)
        halfway = dot(p_ref[at], n_ref[...]).astype(BF16)
        c_ref[at] = dot_t(halfway, p_ref[...]).astype(BF16)

    pair = 2 * rows
    mine = pl.ds(pl.multiple_of(c * half, half), half)
    theirs = pl.ds(pl.multiple_of(other * half, half), half)
    for i, chip in enumerate((x2, xp, xm, x)):
        at = pl.ds(pl.multiple_of(chip * pair, pair), pair)
        conj = c_ref[at]
        square = dot(conj, c_ref[...])
        quintic = (coeff_cubic * conj.astype(F32) + coeff_quintic * square).astype(BF16)
        product = dot(quintic, p_ref[...])
        final = (coeff_linear * p_ref[at].astype(F32) + product).astype(BF16)
        for k in range(chunks):
            u = (dot(final, xc[k]) * scale).astype(BF16)
            ubuf[i, 0, :, cols(k)] = u[:rows]
            ubuf[i, 1, :, cols(k)] = u[rows:]
        if i == 0:
            for d in range(2):
                send(ubuf.at[0, d], uhop.at[d], o_hop.at[0, d], o_hop.at[1, d], x=sides[d], core=c)
        elif i < 3:
            d = i - 1
            for h in range(2):
                send(
                    ubuf.at[i, h], out.at[x, :, mine],
                    o_d1.at[0, d, h], o_d1.at[1, d, c], x=sides[d], core=h,
                )
        else:
            send(ubuf.at[3, other], out.at[x, :, mine], o_p.at[0], o_p.at[1], x=x, core=other)
            stay = pltpu.make_async_copy(ubuf.at[3, c], out.at[x, :, mine], o_own)
            stay.start()
    for d in range(2):
        arrived(uhop.at[d], o_hop.at[1, d], o_hop.at[0, d], x=sides[d], core=c)
        send(uhop.at[d], out.at[came[d], :, mine], o_d2.at[0, d], o_d2.at[1, c], x=sides[d], core=d)
    stay.wait()
    arrived(out.at[x, :, theirs], o_p.at[1], o_p.at[0], x=x, core=other)
    for d in range(2):
        for h in range(2):
            arrived(
                out.at[came[d], :, pl.ds(h * half, half)], o_d1.at[1, d, h], o_d1.at[0, d, h],
                x=sides[d], core=h,
            )
    for h in range(2):
        arrived(out.at[x2, :, pl.ds(h * half, half)], o_d2.at[1, h], o_d2.at[0, h], x=xp, core=h)
    for copy in sent:
        copy.wait_send()


def per_device(mom_values, mom_scale, gradients):
    slots, rows, width = gradients.shape
    half, ff = width // 2, 8 * rows
    chunks = half // WIDTH
    sizes = (lax.axis_size("y"), lax.axis_size("z"))
    entries = float(gradients.size * 8 * sizes[0] * sizes[1])
    near = [max(len(near_offsets(n)), 1) for n in sizes]
    dma = pltpu.SemaphoreType.DMA

    def body(*refs):
        kernel(entries, sizes, *refs)

    return pl.pallas_call(
        body,
        out_shape=jax.ShapeDtypeStruct(mom_values.shape, BF16),
        in_specs=[
            pl.BlockSpec(memory_space=pl.ANY),
            pl.BlockSpec(memory_space=pltpu.VMEM),
            pl.BlockSpec(memory_space=pl.ANY),
        ],
        out_specs=pl.BlockSpec(memory_space=pltpu.VMEM),
        scratch_shapes=[
            pltpu.VMEM((2, slots, rows, half), BF16),
            pltpu.VMEM((2, slots, rows, half), BF16),
            pltpu.VMEM((1, 128), F32),
            pltpu.VMEM((8, 1, 128), F32),
            pltpu.VMEM((1, 128), F32),
            pltpu.VMEM((near[0], 1, 128), F32),
            pltpu.VMEM((1, 128), F32),
            pltpu.VMEM((near[1], 1, 128), F32),
            pltpu.VMEM((2, 1, 128), F32),
            pltpu.VMEM((2, 1, 128), F32),
            pltpu.VMEM((3, 2, slots, rows), F32),
            pltpu.VMEM((3, rows, WIDTH), F32),
            pltpu.VMEM((3, 2, rows, WIDTH), F32),
            pltpu.VMEM((2, 2, rows, half), BF16),
            pltpu.VMEM((2, 2, rows, half), BF16),
            pltpu.VMEM((2, 2, 2, rows, max(RAW, 1) * WIDTH), BF16),
            pltpu.VMEM((chunks, ff, WIDTH), BF16),
            pltpu.VMEM((chunks - RAW, 2, 2, rows, WIDTH), BF16),
            pltpu.VMEM((chunks, rows, WIDTH), BF16),
            pltpu.VMEM((ff, ff), F32),
            pltpu.VMEM((2, ff // 2, ff), BF16),
            pltpu.VMEM((2, ff // 2, ff), BF16),
            pltpu.VMEM((ff, ff), BF16),
            pltpu.VMEM((ff, ff), BF16),
            pltpu.VMEM((ff, ff), BF16),
            pltpu.VMEM((4, 2, rows, half), BF16),
            pltpu.VMEM((2, rows, half), BF16),
            dma((2, 2)),
            dma((2, 8)),
            dma((2, near[0])),
            dma((2, near[1])),
            dma((2, 2)),
            dma((2, 3, 2)),
            dma((2, 2, 2)),
            dma((2, 2, 2)),
            dma((2, 2, 2, 2)),
            dma((2, chunks, 2, 2)),
            dma((2,)),
            dma((2, 2)),
            dma((2, 2)),
            dma((2, 2)),
            dma((2, 2, 2)),
            dma((2,)),
            dma,
        ],
        compiler_params=pltpu.CompilerParams(
            collective_id=0, has_side_effects=True, vmem_limit_bytes=66_000_000
        ),
        name="muon",
    )(mom_values, mom_scale, gradients)


def solution(mesh):
    finer = Mesh(mesh.devices.reshape(4, 2, 8, 16), AXES)
    return jax.shard_map(
        per_device,
        mesh=finer,
        in_specs=(P(EXPERT, ZERO, None), P(EXPERT, ZERO), P(EXPERT, ZERO, None)),
        out_specs=P(EXPERT, ZERO, None),
        check_vma=False,
    )
```

time: 143 us -> 66.5 us (0.47)
  blocking collectives: 114 us -> 0 us
  Pallas kernels: 0 us -> 64 us
  waiting for transfers between devices: 13.3 us -> 0 us
  other arithmetic: 6.19 us -> 0 us
  matrix products: 4.52 us -> 0 us
  starting transfers between devices: 2.51 us -> 0 us
  local copies, waits for them, and re-layouts: 0.27 us -> 2.3 us
  between operations: 1.5 us -> 0.01 us
    psum x4 -> x0, blocking collectives: 66.8 us -> none  [one_axis_at_a_time(): array = lax.psum(array, axis)]
    pallas_call x0 -> x1, Pallas kernels: none -> 64 us  [per_device(): pl.pallas_call(body, out_shape=jax.ShapeDtypeStruct(mom_values.shape, BF1...]
    all_to_all x2 -> x0, blocking collectives: 47.7 us -> none  [the longest x1 28.4 us: per_device(): lax.all_to_all(outgoing, ZERO, split_axis=0, concat_axis=0, tiled=True)]
    ppermute x1 -> x0, waiting for transfers between devices: 13.3 us -> none  [swapped(): lax.ppermute(array, axis, [(i, i ^ 1 << apart) for i in range(lax.axis_si...]
    dot_general x5 -> x0, matrix products: 4.52 us -> none  [the longest x1 2.19 us: final_update(): applied = jnp.dot(polynomial, matrix, preferred_element_type=jnp.float32)]
    reduce_sum x2 -> x0, other arithmetic: 3.12 us -> none  [the longest x1 2.46 us: per_device(): local_sum = jnp.sum(jnp.square(gradients.astype(jnp.float32)))]
    ppermute x1 -> x0, starting transfers between devices: 2.51 us -> none  [swapped(): lax.ppermute(array, axis, [(i, i ^ 1 << apart) for i in range(lax.axis_si...]
    unnamed x6 -> x1, local copies, waits for them, and re-layouts: 0.08 us -> 2.3 us
  transfers between devices with their start and end apart: 1 -> 0, of which waited for: 1 -> 0; matrix products, arithmetic and copies ran while one was open for 0% -> 0% of each run, Pallas kernels for 0% -> 0%
where the time goes in v1:
time: 66.5 us; the launch traced here: 66.3 us
  Pallas kernels  64 us (96%)
  local copies, waits for them, and re-layouts  2.3 us (3%)
    pallas_call x1, Pallas kernels, per_device(): pl.pallas_call(body, out_shape=jax.ShapeDtypeStruct(mom_values.shape, BF1...  64 us
    unnamed x1, local copies, waits for them, and re-layouts  2.3 us

profile of v1, /device:TPU:1, one launch (start us, length us, event | category | flops | bytes accessed | tf_op | source)
XLA Modules:
  0.0 66.3 jit_solution(2220546962519215762)
XLA Ops:
  0.0 64.0 %muon.1 = bf16[4,64,2048]{2,1,0:T(8,128)(2,1)} custom-call(bf16[4,64,2048]{2,1,0:T(8,128)(2,1)} %refs_0_.1, f32[4,64]{1,0:T(4,128)} %refs_1_.1, bf16[4,64,2048]{2,1,0:T(8,128)(2,1)} %refs_2_.1), custom_call_target="tpu_custom_call" | custom-call | tf_op jit(solution)/shard_map/muon/pallas_call | solution.py:343
  64.0 2.3 %copy.5 = bf16[4,64,2048]{2,1,0:T(8,128)(2,1)} copy(bf16[4,64,2048]{2,1,0:T(8,128)(2,1)} %muon.1) | data formatting | bytes 2097152

commit v2 on v1

v2 whole, which is shorter than its diff:
```python
import jax
import jax.numpy as jnp
from jax import lax
from jax.experimental import pallas as pl
from jax.experimental.pallas import tpu as pltpu
from jax.sharding import Mesh
from jax.sharding import PartitionSpec as P

AXES = ("x", "core", "y", "z")
ZERO = ("x", "core")
EXPERT = ("y", "z")

coeff_linear = 3.4445
coeff_cubic = -4.775
coeff_quintic = 2.0315
decay_rate = 0.95
epsilon = 1e-06

WIDTH = 256
REACH = 4

STOP = 0
F32, BF16 = jnp.float32, jnp.bfloat16


def remote(src, dst, send_sem, recv_sem, **where):
    return pltpu.make_async_remote_copy(
        src_ref=src,
        dst_ref=dst,
        send_sem=send_sem,
        recv_sem=recv_sem,
        device_id=where,
        device_id_type=pl.DeviceIdType.MESH,
    )


def arrived(dst, recv_sem, send_sem, **where):
    remote(dst, dst, send_sem, recv_sem, **where).wait_recv()


def dot(a, b):
    return jnp.dot(a, b, preferred_element_type=F32)


def dot_t(a, b):
    return lax.dot_general(a, b, (((1,), (1,)), ((), ())), preferred_element_type=F32)


def near_offsets(n):
    if n <= 2 * REACH:
        return list(range(1, n))
    assert n == 4 * REACH
    return [o * s for o in range(REACH, 0, -1) for s in (1, -1)]


def kernel(
    entries, sizes,
    mv, ms, gr, out,
    gbuf, xs_out, xs_in, ys_out, ys_in, zs_out, zs_in, far_out, far_in, tot,
    ms_own, ms_in, sc, hop, raw, xc, gram, g_out, g_in, n_ref, p_ref, c_ref, ubuf, uhop,
    ready, loc_s, msl_s, xs_s, ys_s, zs_s, far_s, tot_s, ms_s, hop_s, fwd_s, d1_s, mate_s, raw_s, g_s,
    o_hop, o_d2, o_d1, o_p, o_own,
):
    ny, nz = sizes
    slots, rows = gbuf.shape[:2]
    half = raw.shape[3]
    chunks = half // WIDTH
    ff = 8 * rows
    x, c, y, z = (lax.axis_index(a) for a in AXES)
    xp, xm, x2 = lax.rem(x + 1, 4), lax.rem(x + 3, 4), lax.rem(x + 2, 4)
    other = 1 - c
    me = 2 * x + c
    sides = (xp, xm)
    came = (xm, xp)
    y_near, z_near = near_offsets(ny), near_offsets(nz)
    at_y = [lax.rem(y + (o + ny), ny) for o in y_near]
    at_z = [lax.rem(z + (o + nz), nz) for o in z_near]
    z_up, z_down = lax.rem(z + REACH, nz), lax.rem(z + nz - REACH % nz, nz)
    far = nz > 2 * REACH
    at_x = [lax.rem(x + dx, 4) for dx in range(4)]
    from_x = [lax.rem(x + 4 - dx, 4) for dx in range(4)]
    group = [(dx, dc) for dx in (2, 1, 3, 0) for dc in (0, 1) if dx or dc]
    mine = pl.ds(pl.multiple_of(c * half, half), half)
    theirs = pl.ds(pl.multiple_of(other * half, half), half)
    mesh_ids = pl.DeviceIdType.MESH

    def member(dx, dc):
        return {"x": at_x[dx], "core": other if dc else c}

    local = [pltpu.make_async_copy(gr.at[m], gbuf.at[m], loc_s.at[m]) for m in range(slots)]
    for copy in local:
        copy.start()
    barrier = pltpu.get_barrier_semaphore()
    for dx in (2, 1, 3, 0):

        @pl.when((c == 1) | (dx != 0))
        def _():
            pl.semaphore_signal(barrier, inc=1, device_id={"x": at_x[dx], "core": 0}, device_id_type=mesh_ids)

    @pl.when(c == 1)
    def _():
        for t in at_z:
            pl.semaphore_signal(barrier, inc=1, device_id={"z": t}, device_id_type=mesh_ids)
        for t in at_y:
            pl.semaphore_signal(barrier, inc=1, device_id={"y": t}, device_id_type=mesh_ids)

    scales = pltpu.make_async_copy(ms, ms_own, msl_s)
    scales.start()
    for t, src in enumerate((gr, mv)):
        pltpu.make_async_copy(src.at[x, :, mine], raw.at[t, me], raw_s.at[t, me]).start()

    @pl.when(c == 0)
    def _():
        pl.semaphore_wait(barrier, 7)
        pl.semaphore_signal(ready, inc=1, device_id={"core": 1}, device_id_type=mesh_ids)

    acc = None
    for m in range(slots):
        local[m].wait()
        for h in range(2):
            g = gbuf[m, :, h * half : (h + 1) * half].astype(F32)
            part = jnp.sum((g * g).reshape(rows // 8, 8, half), axis=0)
            acc = part if acc is None else acc + part
    lanes = acc[:, :128]
    for i in range(1, half // 128):
        lanes = lanes + acc[:, i * 128 : (i + 1) * 128]
    xs_out[...] = jnp.sum(lanes, axis=0, keepdims=True)

    @pl.when(c == 1)
    def _():
        pl.semaphore_wait(ready, 1)

    to_ones = [remote(xs_out, xs_in.at[2 * dx + c], xs_s.at[0, dx], xs_s.at[1, 2 * dx + c], x=at_x[dx], core=1) for dx in range(4)]
    to_scales = [
        remote(ms_own, ms_in.at[me], ms_s.at[0, 2 * dx + dc], ms_s.at[1, me], **member(dx, dc)) for dx, dc in group
    ]
    bulk = [
        remote(
            src.at[x2, :, pl.ds(d * half, half)], hop.at[t, d, c],
            hop_s.at[0, t, d, 0], hop_s.at[1, t, d, c], x=sides[d], core=0,
        )
        for t, src in enumerate((gr, mv))
        for d in range(2)
    ]
    for t, src in enumerate((gr, mv)):
        bulk.append(remote(src.at[x, :, theirs], raw.at[t, me], mate_s.at[t], raw_s.at[t, me], x=x, core=other))
        bulk.extend(
            remote(
                src.at[sides[d], :, pl.ds(k * half, half)], raw.at[t, me],
                d1_s.at[t, d, k], raw_s.at[t, me], x=sides[d], core=k,
            )
            for d in range(2)
            for k in range(2)
        )
    origin = [[2 * came[d] + k for k in range(2)] for d in range(2)]
    passed = [
        [
            remote(
                hop.at[t, d, k], raw.at[t, origin[d][k]],
                fwd_s.at[t, d, k], raw_s.at[t, origin[d][k]], x=sides[d], core=d,
            )
            for t in range(2)
            for d in range(2)
        ]
        for k in range(2)
    ]
    to_y = [remote(ys_out, ys_in.at[i], ys_s.at[0, i], ys_s.at[1, i], y=t) for i, t in enumerate(at_y)]
    to_z = [remote(zs_out, zs_in.at[i], zs_s.at[0, i], zs_s.at[1, i], z=t) for i, t in enumerate(at_z)]
    to_far = [
        remote(far_out.at[i], far_in.at[i], far_s.at[0, i], far_s.at[1, i], z=t) for i, t in ((0, z_down), (1, z_up))
    ]
    to_mate = remote(tot, tot, tot_s.at[0], tot_s.at[1], core=0)

    def start(copies):
        for copy in copies:
            copy.start()

    start(to_ones[1:])

    @pl.when(c == 0)
    def _():
        to_ones[0].start()

    scales.wait()
    start(to_scales)

    @pl.when((c == 0) | (2 * z < nz))
    def _():
        start(bulk)

    ii = lax.broadcasted_iota(jnp.int32, (rows, rows), 0)
    jj = lax.broadcasted_iota(jnp.int32, (rows, rows), 1)
    mat = lax.broadcasted_iota(jnp.int32, (slots, rows), 0)

    def column(values):
        row = jnp.sum(jnp.where(mat == x, values, 0.0), axis=0, keepdims=True)
        col = jnp.sum(jnp.where(ii == jj, row, 0.0), axis=1, keepdims=True)
        return jnp.broadcast_to(decay_rate * col, (rows, WIDTH))

    def columns():
        for dx, dc in group:
            i, at = 2 * dx + dc, member(dx, dc)
            who = 2 * at["x"] + at["core"]
            arrived(ms_in.at[who], ms_s.at[1, who], ms_s.at[0, i], **at)
            sc[who] = column(ms_in[who])
        sc[me] = column(ms_own[...])

    @pl.when(c == 1)
    def _():
        total = xs_out[...]
        for dx in range(4):
            for k in range(2):
                if dx or not k:
                    i = 2 * dx + k
                    arrived(xs_in.at[i], xs_s.at[1, i], xs_s.at[0, dx], x=from_x[dx], core=k)
                    total = total + xs_in[i]
        pl.semaphore_wait(barrier, len(at_y) + len(at_z))
        if y_near:
            ys_out[...] = total
            start(to_y)
            for i, t in enumerate(at_y):
                arrived(ys_in.at[i], ys_s.at[1, i], ys_s.at[0, i], y=t)
                total = total + ys_in[i]
        if z_near:
            zs_out[...] = total
            start(to_z)

        @pl.when(2 * z >= nz)
        def _():
            start(bulk)

        ahead = behind = None
        for i, (o, t) in enumerate(zip(z_near, at_z)):
            arrived(zs_in.at[i], zs_s.at[1, i], zs_s.at[0, i], z=t)
            total = total + zs_in[i]
            if o < 0:
                ahead = zs_in[i] if ahead is None else ahead + zs_in[i]
            elif o < REACH:
                behind = zs_in[i] if behind is None else behind + zs_in[i]
        if far:
            far_out[0] = ahead
            far_out[1] = behind
            start(to_far)
        columns()
        if far:
            for i, t in ((0, z_up), (1, z_down)):
                arrived(far_in.at[i], far_s.at[1, i], far_s.at[0, i], z=t)
                total = total + far_in[i]
        tot[...] = total
        to_mate.start()

    @pl.when(c == 0)
    def _():
        columns()
        for k in range(2):
            for i, copy in enumerate(passed[k]):
                t, d = i // 2, i % 2
                arrived(hop.at[t, d, k], hop_s.at[1, t, d, k], hop_s.at[0, t, d, 0], x=sides[d], core=0)
                copy.start()
        arrived(tot, tot_s.at[1], tot_s.at[0], core=1)

    clip = lax.rsqrt(jnp.sum(tot[...], axis=1, keepdims=True) / entries + epsilon)
    sent = to_ones[1:] + to_scales + bulk

    def send(*args, **where):
        copy = remote(*args, **where)
        copy.start()
        sent.append(copy)

    def finish():
        for copy in sent:
            copy.wait_send()

        @pl.when(c == 0)
        def _():
            for copy in to_ones[:1] + passed[0] + passed[1]:
                copy.wait_send()

        @pl.when(c == 1)
        def _():
            for copy in to_y + to_z + (to_far if far else []) + [to_mate]:
                copy.wait_send()

    if STOP == 4:
        for t in range(2):
            pltpu.make_async_copy(raw.at[t, me], raw.at[t, me], raw_s.at[t, me]).wait()
        out[0, :8, :128] = jnp.broadcast_to(clip, (8, 128)).astype(BF16)
        for i in range(8):
            for t in range(2):
                @pl.when(me != i)
                def _():
                    arrived(raw.at[t, i], raw_s.at[t, i], mate_s.at[t], x=xp, core=c)
        finish()
        return
    for i in range(8):
        for t in range(2):
            arrived(raw.at[t, i], raw_s.at[t, i], mate_s.at[t], x=xp, core=c)
    if STOP == 1:
        out[0, :8, :128] = jnp.broadcast_to(clip, (8, 128)).astype(BF16)
        finish()
        return

    tall = ff // 2
    for k in range(chunks):
        at = pl.ds(k * WIDTH, WIDTH)
        for i in range(8):
            xc[k, pl.ds(i * rows, rows)] = (
                raw[1, i, :, at].astype(F32) * sc[i] + clip * raw[0, i, :, at].astype(F32)
            ).astype(BF16)
        for r in range(2):
            part = dot_t(xc[k, pl.ds(r * tall, tall)], xc[k])
            if k:
                part = gram[pl.ds(r * tall, tall)] + part
            gram[pl.ds(r * tall, tall)] = part
            if k == chunks - 1:
                g_out[r] = part.astype(BF16)
                send(g_out.at[r], g_in.at[r], g_s.at[0, r], g_s.at[1, r], x=x, core=other)
    norm = None
    diag = lax.broadcasted_iota(jnp.int32, (128, 128), 0) == lax.broadcasted_iota(jnp.int32, (128, 128), 1)
    for r in range(2):
        arrived(g_in.at[r], g_s.at[1, r], g_s.at[0, r], x=x, core=other)
        whole = gram[pl.ds(r * tall, tall)] + g_in[r].astype(F32)
        gram[pl.ds(r * tall, tall)] = whole
        for b in range(tall // 128):
            square = whole[b * 128 : (b + 1) * 128, r * tall + b * 128 : r * tall + (b + 1) * 128]
            masked = jnp.where(diag, square, 0.0)
            norm = masked if norm is None else norm + masked
    norm = jnp.sum(jnp.sum(norm, axis=0, keepdims=True), axis=1, keepdims=True) + epsilon
    inverse = 1.0 / norm
    scale = (2.0 * half) ** 0.5 * lax.rsqrt(norm)

    if STOP == 2:
        out[0, :8, :128] = jnp.broadcast_to(inverse, (8, 128)).astype(BF16)
        finish()
        return
    for r in range(2):
        at = pl.ds(r * tall, tall)
        n_ref[at] = (gram[at] * inverse).astype(BF16)
    for r in range(2):
        at = pl.ds(r * tall, tall)
        eye = lax.broadcasted_iota(jnp.int32, (tall, ff), 0) + r * tall == lax.broadcasted_iota(jnp.int32, (tall, ff), 1)
        square = dot(n_ref[at], n_ref[...])
        p_ref[at] = (
            jnp.where(eye, coeff_linear, 0.0) + coeff_cubic * n_ref[at].astype(F32) + coeff_quintic * square
        ).astype(BF16)
    for r in range(2):
        at = pl.ds(r * tall, tall)
        halfway = dot(p_ref[at], n_ref[...]).astype(BF16)
        c_ref[at] = dot_t(halfway, p_ref[...]).astype(BF16)

    if STOP == 3:
        out[0, :8, :128] = (c_ref[:8, :128].astype(F32) * scale).astype(BF16)
        finish()
        return
    pair = 2 * rows

    def cols(k):
        return pl.ds(k * WIDTH, WIDTH)

    for i, chip in enumerate((x2, xp, xm, x)):
        at = pl.ds(pl.multiple_of(chip * pair, pair), pair)
        conj = c_ref[at]
        square = dot(conj, c_ref[...])
        quintic = (coeff_cubic * conj.astype(F32) + coeff_quintic * square).astype(BF16)
        product = dot(quintic, p_ref[...])
        final = (coeff_linear * p_ref[at].astype(F32) + product).astype(BF16)
        for k in range(chunks):
            u = (dot(final, xc[k]) * scale).astype(BF16)
            ubuf[i, 0, :, cols(k)] = u[:rows]
            ubuf[i, 1, :, cols(k)] = u[rows:]
        if i == 0:
            for d in range(2):
                send(ubuf.at[0, d], uhop.at[d], o_hop.at[0, d], o_hop.at[1, d], x=sides[d], core=c)
        elif i < 3:
            d = i - 1
            for h in range(2):
                send(
                    ubuf.at[i, h], out.at[x, :, mine],
                    o_d1.at[0, d, h], o_d1.at[1, d, c], x=sides[d], core=h,
                )
        else:
            send(ubuf.at[3, other], out.at[x, :, mine], o_p.at[0], o_p.at[1], x=x, core=other)
            stay = pltpu.make_async_copy(ubuf.at[3, c], out.at[x, :, mine], o_own)
            stay.start()
    for d in range(2):
        arrived(uhop.at[d], o_hop.at[1, d], o_hop.at[0, d], x=sides[d], core=c)
        send(uhop.at[d], out.at[came[d], :, mine], o_d2.at[0, d], o_d2.at[1, c], x=sides[d], core=d)
    stay.wait()
    arrived(out.at[x, :, theirs], o_p.at[1], o_p.at[0], x=x, core=other)
    for d in range(2):
        for h in range(2):
            arrived(
                out.at[came[d], :, pl.ds(h * half, half)], o_d1.at[1, d, h], o_d1.at[0, d, h],
                x=sides[d], core=h,
            )
    for h in range(2):
        arrived(out.at[x2, :, pl.ds(h * half, half)], o_d2.at[1, h], o_d2.at[0, h], x=xp, core=h)
    finish()


def per_device(mom_values, mom_scale, gradients):
    slots, rows, width = gradients.shape
    half, ff = width // 2, 8 * rows
    chunks = half // WIDTH
    sizes = (lax.axis_size("y"), lax.axis_size("z"))
    entries = float(gradients.size * 8 * sizes[0] * sizes[1])
    near = [max(len(near_offsets(n)), 1) for n in sizes]
    dma = pltpu.SemaphoreType.DMA

    def body(*refs):
        kernel(entries, sizes, *refs)

    return pl.pallas_call(
        body,
        out_shape=jax.ShapeDtypeStruct(mom_values.shape, BF16),
        in_specs=[pl.BlockSpec(memory_space=pltpu.HBM)] * 3,
        out_specs=pl.BlockSpec(memory_space=pltpu.VMEM),
        scratch_shapes=[
            pltpu.VMEM((slots, rows, width), BF16),
            pltpu.VMEM((1, 128), F32),
            pltpu.VMEM((8, 1, 128), F32),
            pltpu.VMEM((1, 128), F32),
            pltpu.VMEM((near[0], 1, 128), F32),
            pltpu.VMEM((1, 128), F32),
            pltpu.VMEM((near[1], 1, 128), F32),
            pltpu.VMEM((2, 1, 128), F32),
            pltpu.VMEM((2, 1, 128), F32),
            pltpu.VMEM((1, 128), F32),
            pltpu.VMEM((slots, rows), F32),
            pltpu.VMEM((8, slots, rows), F32),
            pltpu.VMEM((8, rows, WIDTH), F32),
            pltpu.VMEM((2, 2, 2, rows, half), BF16),
            pltpu.VMEM((2, 8, rows, half), BF16),
            pltpu.VMEM((chunks, ff, WIDTH), BF16),
            pltpu.VMEM((ff, ff), F32),
            pltpu.VMEM((2, ff // 2, ff), BF16),
            pltpu.VMEM((2, ff // 2, ff), BF16),
            pltpu.VMEM((ff, ff), BF16),
            pltpu.VMEM((ff, ff), BF16),
            pltpu.VMEM((ff, ff), BF16),
            pltpu.VMEM((4, 2, rows, half), BF16),
            pltpu.VMEM((2, rows, half), BF16),
            pltpu.SemaphoreType.REGULAR,
            dma((slots,)),
            dma,
            dma((2, 8)),
            dma((2, near[0])),
            dma((2, near[1])),
            dma((2, 2)),
            dma((2,)),
            dma((2, 8)),
            dma((2, 2, 2, 2)),
            dma((2, 2, 2)),
            dma((2, 2, 2)),
            dma((2,)),
            dma((2, 8)),
            dma((2, 2)),
            dma((2, 2)),
            dma((2, 2)),
            dma((2, 2, 2)),
            dma((2,)),
            dma,
        ],
        compiler_params=pltpu.CompilerParams(
            collective_id=0, has_side_effects=True, vmem_limit_bytes=66_000_000
        ),
        name="muon",
    )(mom_values, mom_scale, gradients)


def solution(mesh):
    finer = Mesh(mesh.devices.reshape(4, 2, 8, 16), AXES)
    return jax.shard_map(
        per_device,
        mesh=finer,
        in_specs=(P(EXPERT, ZERO, None), P(EXPERT, ZERO), P(EXPERT, ZERO, None)),
        out_specs=P(EXPERT, ZERO, None),
        check_vma=False,
    )
```

time: 66.5 us -> 62.2 us (0.935)
  Pallas kernels: 64 us -> 59.7 us
    pallas_call x1, Pallas kernels: 64 us -> 59.7 us  [per_device(): pl.pallas_call(body, out_shape=jax.ShapeDtypeStruct(mom_values.shape, BF1...]
where the time goes in v2:
time: 62.2 us; the launch traced here: 62 us
  Pallas kernels  59.7 us (96%)
  local copies, waits for them, and re-layouts  2.3 us (4%)
    pallas_call x1, Pallas kernels, per_device(): pl.pallas_call(body, out_shape=jax.ShapeDtypeStruct(mom_values.shape, BF1...  59.7 us
    unnamed x1, local copies, waits for them, and re-layouts  2.3 us

profile of v2, /device:TPU:1, one launch (start us, length us, event | category | flops | bytes accessed | tf_op | source)
XLA Modules:
  0.0 62.0 jit_solution(16964712215467470323)
XLA Ops:
  0.0 59.7 %muon.1 = bf16[4,64,2048]{2,1,0:T(8,128)(2,1)} custom-call(bf16[4,64,2048]{2,1,0:T(8,128)(2,1)} %refs_0_.1, f32[4,64]{1,0:T(4,128)} %refs_1_.1, bf16[4,64,2048]{2,1,0:T(8,128)(2,1)} %refs_2_.1), custom_call_target="tpu_custom_call" | custom-call | tf_op jit(solution)/shard_map/muon/pallas_call | solution.py:413
  59.7 2.3 %copy.5 = bf16[4,64,2048]{2,1,0:T(8,128)(2,1)} copy(bf16[4,64,2048]{2,1,0:T(8,128)(2,1)} %muon.1) | data formatting | bytes 2097152

commit v3 on v2

--- a/solution.py
+++ b/solution.py
@@ -17,9 +17,8 @@
 epsilon = 1e-06
 
 WIDTH = 256
+STOP = 0
 REACH = 4
-
-STOP = 0
 F32, BF16 = jnp.float32, jnp.bfloat16
 
 
@@ -46,11 +45,11 @@
     return lax.dot_general(a, b, (((1,), (1,)), ((), ())), preferred_element_type=F32)
 
 
-def near_offsets(n):
-    if n <= 2 * REACH:
-        return list(range(1, n))
-    assert n == 4 * REACH
-    return [o * s for o in range(REACH, 0, -1) for s in (1, -1)]
+def far_first(n):
+    if n > 2 * REACH:
+        assert n == 4 * REACH
+        return [o * s for o in range(REACH, 0, -1) for s in (1, -1)]
+    return sorted(range(1, n), key=lambda o: -min(o, n - o))
 
 
 def kernel(
@@ -58,7 +57,7 @@
     mv, ms, gr, out,
     gbuf, xs_out, xs_in, ys_out, ys_in, zs_out, zs_in, far_out, far_in, tot,
     ms_own, ms_in, sc, hop, raw, xc, gram, g_out, g_in, n_ref, p_ref, c_ref, ubuf, uhop,
-    ready, loc_s, msl_s, xs_s, ys_s, zs_s, far_s, tot_s, ms_s, hop_s, fwd_s, d1_s, mate_s, raw_s, g_s,
+    ready, late, loc_s, msl_s, xs_s, ys_s, zs_s, far_s, tot_s, ms_s, hop_s, fwd_s, d1_s, mate_s, raw_s, g_s,
     o_hop, o_d2, o_d1, o_p, o_own,
 ):
     ny, nz = sizes
@@ -72,7 +71,7 @@
     me = 2 * x + c
     sides = (xp, xm)
     came = (xm, xp)
-    y_near, z_near = near_offsets(ny), near_offsets(nz)
+    y_near, z_near = far_first(ny), far_first(nz)
     at_y = [lax.rem(y + (o + ny), ny) for o in y_near]
     at_z = [lax.rem(z + (o + nz), nz) for o in z_near]
     z_up, z_down = lax.rem(z + REACH, nz), lax.rem(z + nz - REACH % nz, nz)
@@ -87,16 +86,16 @@
     def member(dx, dc):
         return {"x": at_x[dx], "core": other if dc else c}
 
+    barrier = pltpu.get_barrier_semaphore()
+    for dx in (2, 1, 3, 0):
+
+        @pl.when(((c == 1) | (dx != 0)) & (me != 0))
+        def _():
+            pl.semaphore_signal(barrier, inc=1, device_id={"x": at_x[dx], "core": 0}, device_id_type=mesh_ids)
+
     local = [pltpu.make_async_copy(gr.at[m], gbuf.at[m], loc_s.at[m]) for m in range(slots)]
     for copy in local:
         copy.start()
-    barrier = pltpu.get_barrier_semaphore()
-    for dx in (2, 1, 3, 0):
-
-        @pl.when((c == 1) | (dx != 0))
-        def _():
-            pl.semaphore_signal(barrier, inc=1, device_id={"x": at_x[dx], "core": 0}, device_id_type=mesh_ids)
-
     @pl.when(c == 1)
     def _():
         for t in at_z:
@@ -111,8 +110,20 @@
 
     @pl.when(c == 0)
     def _():
-        pl.semaphore_wait(barrier, 7)
-        pl.semaphore_signal(ready, inc=1, device_id={"core": 1}, device_id_type=mesh_ids)
+        pl.semaphore_wait(barrier, jnp.where(x == 0, 7, 6))
+
+        @pl.when(x == 0)
+        def _():
+            for dx, dc in group:
+                pl.semaphore_signal(late, inc=1, device_id=member(dx, dc), device_id_type=mesh_ids)
+
+        @pl.when(x != 0)
+        def _():
+            pl.semaphore_signal(ready, inc=1, device_id={"core": 1}, device_id_type=mesh_ids)
+
+        @pl.when(x == 1)
+        def _():
+            pl.semaphore_signal(ready, inc=1, device_id={"x": xm, "core": 1}, device_id_type=mesh_ids)
 
     acc = None
     for m in range(slots):
@@ -132,26 +143,33 @@
 
     to_ones = [remote(xs_out, xs_in.at[2 * dx + c], xs_s.at[0, dx], xs_s.at[1, 2 * dx + c], x=at_x[dx], core=1) for dx in range(4)]
     to_scales = [
-        remote(ms_own, ms_in.at[me], ms_s.at[0, 2 * dx + dc], ms_s.at[1, me], **member(dx, dc)) for dx, dc in group
+        (
+            remote(ms_own, ms_in.at[me], ms_s.at[0, 2 * dx + dc], ms_s.at[1, me], **member(dx, dc)),
+            (at_x[dx] == 0) & ((c == 1) if dc else (c == 0)),
+        )
+        for dx, dc in group
     ]
     bulk = [
-        remote(
-            src.at[x2, :, pl.ds(d * half, half)], hop.at[t, d, c],
-            hop_s.at[0, t, d, 0], hop_s.at[1, t, d, c], x=sides[d], core=0,
+        (
+            remote(
+                src.at[x2, :, pl.ds(d * half, half)], hop.at[t, d, c],
+                hop_s.at[0, t, d, 0], hop_s.at[1, t, d, c], x=sides[d], core=0,
+            ),
+            sides[d] == 0,
         )
         for t, src in enumerate((gr, mv))
         for d in range(2)
     ]
     for t, src in enumerate((gr, mv)):
-        bulk.append(remote(src.at[x, :, theirs], raw.at[t, me], mate_s.at[t], raw_s.at[t, me], x=x, core=other))
-        bulk.extend(
-            remote(
-                src.at[sides[d], :, pl.ds(k * half, half)], raw.at[t, me],
-                d1_s.at[t, d, k], raw_s.at[t, me], x=sides[d], core=k,
-            )
-            for d in range(2)
-            for k in range(2)
-        )
+        mate = remote(src.at[x, :, theirs], raw.at[t, me], mate_s.at[t], raw_s.at[t, me], x=x, core=other)
+        bulk.append((mate, me == 1))
+        for d in range(2):
+            for k in range(2):
+                copy = remote(
+                    src.at[sides[d], :, pl.ds(k * half, half)], raw.at[t, me],
+                    d1_s.at[t, d, k], raw_s.at[t, me], x=sides[d], core=k,
+                )
+                bulk.append((copy, sides[d] == 0 if k == 0 else None))
     origin = [[2 * came[d] + k for k in range(2)] for d in range(2)]
     passed = [
         [
@@ -175,6 +193,23 @@
         for copy in copies:
             copy.start()
 
+    def start_known(copies):
+        for copy, to_late in copies:
+            if to_late is None:
+                copy.start()
+            else:
+                pl.when(jnp.logical_not(to_late))(copy.start)
+
+    def start_late(copies):
+        for copy, to_late in copies:
+            if to_late is not None:
+                pl.when(to_late)(copy.start)
+
+    def wait_late():
+        @pl.when(me != 0)
+        def _():
+            pl.semaphore_wait(late, 1)
+
     start(to_ones[1:])
 
     @pl.when(c == 0)
@@ -182,11 +217,11 @@
         to_ones[0].start()
 
     scales.wait()
-    start(to_scales)
+    start_known(to_scales)
 
     @pl.when((c == 0) | (2 * z < nz))
     def _():
-        start(bulk)
+        start_known(bulk)
 
     ii = lax.broadcasted_iota(jnp.int32, (rows, rows), 0)
     jj = lax.broadcasted_iota(jnp.int32, (rows, rows), 1)
@@ -221,13 +256,19 @@
             for i, t in enumerate(at_y):
                 arrived(ys_in.at[i], ys_s.at[1, i], ys_s.at[0, i], y=t)
                 total = total + ys_in[i]
-        if z_near:
-            zs_out[...] = total
-            start(to_z)
+        zs_out[...] = total
+        start(to_z)
+
+        wait_late()
+        start_late(to_scales)
+
+        @pl.when(2 * z < nz)
+        def _():
+            start_late(bulk)
 
         @pl.when(2 * z >= nz)
         def _():
-            start(bulk)
+            start([copy for copy, _ in bulk])
 
         ahead = behind = None
         for i, (o, t) in enumerate(zip(z_near, at_z)):
@@ -251,6 +292,8 @@
 
     @pl.when(c == 0)
     def _():
+        wait_late()
+        start_late(to_scales + bulk)
         columns()
         for k in range(2):
             for i, copy in enumerate(passed[k]):
@@ -260,7 +303,7 @@
         arrived(tot, tot_s.at[1], tot_s.at[0], core=1)
 
     clip = lax.rsqrt(jnp.sum(tot[...], axis=1, keepdims=True) / entries + epsilon)
-    sent = to_ones[1:] + to_scales + bulk
+    sent = to_ones[1:] + [copy for copy, _ in to_scales + bulk]
 
     def send(*args, **where):
         copy = remote(*args, **where)
@@ -404,7 +447,7 @@
     chunks = half // WIDTH
     sizes = (lax.axis_size("y"), lax.axis_size("z"))
     entries = float(gradients.size * 8 * sizes[0] * sizes[1])
-    near = [max(len(near_offsets(n)), 1) for n in sizes]
+    near = [max(len(far_first(n)), 1) for n in sizes]
     dma = pltpu.SemaphoreType.DMA
 
     def body(*refs):
@@ -441,6 +484,7 @@
             pltpu.VMEM((4, 2, rows, half), BF16),
             pltpu.VMEM((2, rows, half), BF16),
             pltpu.SemaphoreType.REGULAR,
+            pltpu.SemaphoreType.REGULAR,
             dma((slots,)),
             dma,
             dma((2, 8)),
@@ -462,7 +506,7 @@
             dma,
         ],
         compiler_params=pltpu.CompilerParams(
-            collective_id=0, has_side_effects=True, vmem_limit_bytes=66_000_000
+            collective_id=0, has_side_effects=True, vmem_limit_bytes=55_200_000
         ),
         name="muon",
     )(mom_values, mom_scale, gradients)

time: 62.2 us -> 57.4 us (0.923)
  Pallas kernels: 59.7 us -> 55.6 us
  local copies, waits for them, and re-layouts: 2.3 us -> 1.65 us
    pallas_call x1, Pallas kernels: 59.7 us -> 55.6 us  [per_device(): pl.pallas_call(body, out_shape=jax.ShapeDtypeStruct(mom_values.shape, BF1...]
    unnamed x1 -> x3, local copies, waits for them, and re-layouts: 2.3 us -> 1.65 us
where the time goes in v3:
time: 57.4 us; the launch traced here: 57.3 us
  Pallas kernels  55.6 us (97%)
  local copies, waits for them, and re-layouts  1.65 us (3%)
    pallas_call x1, Pallas kernels, per_device(): pl.pallas_call(body, out_shape=jax.ShapeDtypeStruct(mom_values.shape, BF1...  55.6 us
    unnamed x3, local copies, waits for them, and re-layouts  1.65 us

profile of v3, /device:TPU:1, one launch (start us, length us, event | category | flops | bytes accessed | tf_op | source)
XLA Modules:
  0.0 57.3 jit_solution(13778208207189846513)
XLA Ops:
  0.0 0.0 copy-start
  0.0 0.7 %copy-done = f32[4,64]{1,0:T(4,128)S(1)} copy-done((f32[4,64]{1,0:T(4,128)S(1)}, f32[4,64]{1,0:T(4,128)}, u32[]{:S(2)}) %copy-start) | copy-done | bytes 1048
  0.7 55.6 %muon.1 = bf16[4,64,2048]{2,1,0:T(8,128)(2,1)S(1)} custom-call(bf16[4,64,2048]{2,1,0:T(8,128)(2,1)} %refs_0_.1, f32[4,64]{1,0:T(4,128)S(1)} %copy-done, bf16[4,64,2048]{2,1,0:T(8,128)(2,1)} %refs_2_.1), custom_call_target="tpu_custom_call" | custom-call | tf_op jit(solution)/shard_map/muon/pallas_call | solution.py:456
  56.3 1.0 %copy.5 = bf16[4,64,2048]{2,1,0:T(8,128)(2,1)} copy(bf16[4,64,2048]{2,1,0:T(8,128)(2,1)S(1)} %muon.1) | data formatting | bytes 2097152
Async XLA Ops:
  0.0 0.7 %copy-start = (f32[4,64]{1,0:T(4,128)S(1)}, f32[4,64]{1,0:T(4,128)}, u32[]{:S(2)}) copy-start(f32[4,64]{1,0:T(4,128)} %refs_1_.1) | copy-start | bytes 3076

commit v4 on v3

--- a/solution.py
+++ b/solution.py
@@ -17,7 +17,6 @@
 epsilon = 1e-06
 
 WIDTH = 256
-STOP = 0
 REACH = 4
 F32, BF16 = jnp.float32, jnp.bfloat16
 
@@ -56,9 +55,9 @@
     entries, sizes,
     mv, ms, gr, out,
     gbuf, xs_out, xs_in, ys_out, ys_in, zs_out, zs_in, far_out, far_in, tot,
-    ms_own, ms_in, sc, hop, raw, xc, gram, g_out, g_in, n_ref, p_ref, c_ref, ubuf, uhop,
-    ready, late, loc_s, msl_s, xs_s, ys_s, zs_s, far_s, tot_s, ms_s, hop_s, fwd_s, d1_s, mate_s, raw_s, g_s,
-    o_hop, o_d2, o_d1, o_p, o_own,
+    ms_own, ms_in, sc, hop, raw, xc, gram, g_out, g_in, n_ref, p_ref, c_ref, ubuf, uhop, counted,
+    ready, late, loc_s, msl_s, sum_send, xs_s, ys_s, zs_s, far_s, tot_s, ms_send, ms_s, bulk_send, hop_s, fwd_send,
+    raw_s, g_s, o_send, o_mate, o_hop, o_s,
 ):
     ny, nz = sizes
     slots, rows = gbuf.shape[:2]
@@ -96,6 +95,13 @@
     local = [pltpu.make_async_copy(gr.at[m], gbuf.at[m], loc_s.at[m]) for m in range(slots)]
     for copy in local:
         copy.start()
+    if far:
+
+        @pl.when(c == 0)
+        def _():
+            for t in (z_up, z_down):
+                pl.semaphore_signal(barrier, inc=1, device_id={"z": t, "core": 1}, device_id_type=mesh_ids)
+
     @pl.when(c == 1)
     def _():
         for t in at_z:
@@ -105,8 +111,9 @@
 
     scales = pltpu.make_async_copy(ms, ms_own, msl_s)
     scales.start()
+    pltpu.make_async_copy(ms, ms_in.at[me], ms_s).start()
     for t, src in enumerate((gr, mv)):
-        pltpu.make_async_copy(src.at[x, :, mine], raw.at[t, me], raw_s.at[t, me]).start()
+        pltpu.make_async_copy(src.at[x, :, mine], raw.at[t, me], raw_s).start()
 
     @pl.when(c == 0)
     def _():
@@ -141,10 +148,10 @@
     def _():
         pl.semaphore_wait(ready, 1)
 
-    to_ones = [remote(xs_out, xs_in.at[2 * dx + c], xs_s.at[0, dx], xs_s.at[1, 2 * dx + c], x=at_x[dx], core=1) for dx in range(4)]
+    to_ones = [remote(xs_out, xs_in.at[2 * ((dx + 3) % 4) + c], sum_send, xs_s, x=at_x[dx], core=1) for dx in range(4)]
     to_scales = [
         (
-            remote(ms_own, ms_in.at[me], ms_s.at[0, 2 * dx + dc], ms_s.at[1, me], **member(dx, dc)),
+            remote(ms_own, ms_in.at[me], ms_send, ms_s, **member(dx, dc)),
             (at_x[dx] == 0) & ((c == 1) if dc else (c == 0)),
         )
         for dx, dc in group
@@ -153,7 +160,7 @@
         (
             remote(
                 src.at[x2, :, pl.ds(d * half, half)], hop.at[t, d, c],
-                hop_s.at[0, t, d, 0], hop_s.at[1, t, d, c], x=sides[d], core=0,
+                bulk_send, hop_s.at[c], x=sides[d], core=0,
             ),
             sides[d] == 0,
         )
@@ -161,13 +168,13 @@
         for d in range(2)
     ]
     for t, src in enumerate((gr, mv)):
-        mate = remote(src.at[x, :, theirs], raw.at[t, me], mate_s.at[t], raw_s.at[t, me], x=x, core=other)
+        mate = remote(src.at[x, :, theirs], raw.at[t, me], bulk_send, raw_s, x=x, core=other)
         bulk.append((mate, me == 1))
         for d in range(2):
             for k in range(2):
                 copy = remote(
                     src.at[sides[d], :, pl.ds(k * half, half)], raw.at[t, me],
-                    d1_s.at[t, d, k], raw_s.at[t, me], x=sides[d], core=k,
+                    bulk_send, raw_s, x=sides[d], core=k,
                 )
                 bulk.append((copy, sides[d] == 0 if k == 0 else None))
     origin = [[2 * came[d] + k for k in range(2)] for d in range(2)]
@@ -175,19 +182,21 @@
         [
             remote(
                 hop.at[t, d, k], raw.at[t, origin[d][k]],
-                fwd_s.at[t, d, k], raw_s.at[t, origin[d][k]], x=sides[d], core=d,
+                fwd_send, raw_s, x=sides[d], core=d,
             )
             for t in range(2)
             for d in range(2)
         ]
         for k in range(2)
     ]
-    to_y = [remote(ys_out, ys_in.at[i], ys_s.at[0, i], ys_s.at[1, i], y=t) for i, t in enumerate(at_y)]
-    to_z = [remote(zs_out, zs_in.at[i], zs_s.at[0, i], zs_s.at[1, i], z=t) for i, t in enumerate(at_z)]
+    to_y = [remote(ys_out, ys_in.at[i], sum_send, ys_s, y=t) for i, t in enumerate(at_y)]
+    to_z = [remote(zs_out, zs_in.at[i], sum_send, zs_s, z=t) for i, t in enumerate(at_z)]
     to_far = [
-        remote(far_out.at[i], far_in.at[i], far_s.at[0, i], far_s.at[1, i], z=t) for i, t in ((0, z_down), (1, z_up))
+        remote(far_out.at[i], far_in.at[i], sum_send, far_s, z=t, core=k)
+        for i, t in ((0, z_down), (1, z_up))
+        for k in range(2)
     ]
-    to_mate = remote(tot, tot, tot_s.at[0], tot_s.at[1], core=0)
+    to_mate = remote(tot, tot, sum_send, tot_s, core=0)
 
     def start(copies):
         for copy in copies:
@@ -233,46 +242,37 @@
         return jnp.broadcast_to(decay_rate * col, (rows, WIDTH))
 
     def columns():
-        for dx, dc in group:
-            i, at = 2 * dx + dc, member(dx, dc)
-            who = 2 * at["x"] + at["core"]
-            arrived(ms_in.at[who], ms_s.at[1, who], ms_s.at[0, i], **at)
-            sc[who] = column(ms_in[who])
-        sc[me] = column(ms_own[...])
+        arrived(ms_in, ms_s, ms_send, core=other)
+        for i in range(8):
+            sc[i] = column(ms_in[i])
 
     @pl.when(c == 1)
     def _():
         total = xs_out[...]
-        for dx in range(4):
-            for k in range(2):
-                if dx or not k:
-                    i = 2 * dx + k
-                    arrived(xs_in.at[i], xs_s.at[1, i], xs_s.at[0, dx], x=from_x[dx], core=k)
-                    total = total + xs_in[i]
-        pl.semaphore_wait(barrier, len(at_y) + len(at_z))
+        arrived(xs_in.at[pl.ds(0, 7)], xs_s, sum_send, core=0)
+        for i in range(7):
+            total = total + xs_in[i]
+        wait_late()
+        start_late(to_scales)
+
+        @pl.when(2 * z < nz)
+        def _():
+            start_late(bulk)
+
+        pl.semaphore_wait(barrier, len(at_y) + len(at_z) + (2 if far else 0))
         if y_near:
             ys_out[...] = total
             start(to_y)
-            for i, t in enumerate(at_y):
-                arrived(ys_in.at[i], ys_s.at[1, i], ys_s.at[0, i], y=t)
+            arrived(ys_in, ys_s, sum_send, y=at_y[0])
+            for i in range(len(at_y)):
                 total = total + ys_in[i]
         zs_out[...] = total
         start(to_z)
 
-        wait_late()
-        start_late(to_scales)
-
-        @pl.when(2 * z < nz)
-        def _():
-            start_late(bulk)
-
-        @pl.when(2 * z >= nz)
-        def _():
-            start([copy for copy, _ in bulk])
-
         ahead = behind = None
-        for i, (o, t) in enumerate(zip(z_near, at_z)):
-            arrived(zs_in.at[i], zs_s.at[1, i], zs_s.at[0, i], z=t)
+        if z_near:
+            arrived(zs_in, zs_s, sum_send, z=at_z[0])
+        for i, o in enumerate(z_near):
             total = total + zs_in[i]
             if o < 0:
                 ahead = zs_in[i] if ahead is None else ahead + zs_in[i]
@@ -282,66 +282,58 @@
             far_out[0] = ahead
             far_out[1] = behind
             start(to_far)
-        columns()
-        if far:
-            for i, t in ((0, z_up), (1, z_down)):
-                arrived(far_in.at[i], far_s.at[1, i], far_s.at[0, i], z=t)
-                total = total + far_in[i]
         tot[...] = total
         to_mate.start()
 
+        @pl.when(2 * z >= nz)
+        def _():
+            start([copy for copy, _ in bulk])
+
+        columns()
+
     @pl.when(c == 0)
     def _():
         wait_late()
-        start_late(to_scales + bulk)
+        start_late(to_scales)
+
+        start_late(bulk)
         columns()
         for k in range(2):
-            for i, copy in enumerate(passed[k]):
-                t, d = i // 2, i % 2
-                arrived(hop.at[t, d, k], hop_s.at[1, t, d, k], hop_s.at[0, t, d, 0], x=sides[d], core=0)
-                copy.start()
-        arrived(tot, tot_s.at[1], tot_s.at[0], core=1)
-
-    clip = lax.rsqrt(jnp.sum(tot[...], axis=1, keepdims=True) / entries + epsilon)
-    sent = to_ones[1:] + [copy for copy, _ in to_scales + bulk]
+            arrived(hop.at[:, :, k], hop_s.at[k], bulk_send, x=xp, core=0)
+            start(passed[k])
+        arrived(tot, tot_s, sum_send, core=1)
+
+    total = tot[...]
+    if far:
+        arrived(far_in, far_s, sum_send, z=z_up, core=1)
+        total = total + far_in[0] + far_in[1]
+    clip = lax.rsqrt(jnp.sum(total, axis=1, keepdims=True) / entries + epsilon)
+    sent = []
 
     def send(*args, **where):
         copy = remote(*args, **where)
         copy.start()
         sent.append(copy)
 
+    def gone(src, send_sem):
+        remote(src, src, send_sem, raw_s, core=other).wait_send()
+
     def finish():
         for copy in sent:
             copy.wait_send()
+        gone(ms_in.at[pl.ds(0, 7)], ms_send)
+        gone(raw.at[:, pl.ds(0, 7)], bulk_send)
 
         @pl.when(c == 0)
         def _():
-            for copy in to_ones[:1] + passed[0] + passed[1]:
-                copy.wait_send()
+            gone(raw.at[:, pl.ds(0, 4)], fwd_send)
+            gone(xs_in.at[pl.ds(0, 4)], sum_send)
 
         @pl.when(c == 1)
         def _():
-            for copy in to_y + to_z + (to_far if far else []) + [to_mate]:
-                copy.wait_send()
-
-    if STOP == 4:
-        for t in range(2):
-            pltpu.make_async_copy(raw.at[t, me], raw.at[t, me], raw_s.at[t, me]).wait()
-        out[0, :8, :128] = jnp.broadcast_to(clip, (8, 128)).astype(BF16)
-        for i in range(8):
-            for t in range(2):
-                @pl.when(me != i)
-                def _():
-                    arrived(raw.at[t, i], raw_s.at[t, i], mate_s.at[t], x=xp, core=c)
-        finish()
-        return
-    for i in range(8):
-        for t in range(2):
-            arrived(raw.at[t, i], raw_s.at[t, i], mate_s.at[t], x=xp, core=c)
-    if STOP == 1:
-        out[0, :8, :128] = jnp.broadcast_to(clip, (8, 128)).astype(BF16)
-        finish()
-        return
+            gone(counted.at[pl.ds(0, 4 + len(at_y) + len(at_z) + (4 if far else 0))], sum_send)
+
+    arrived(raw, raw_s, bulk_send, core=other)
 
     tall = ff // 2
     for k in range(chunks):
@@ -351,34 +343,35 @@
                 raw[1, i, :, at].astype(F32) * sc[i] + clip * raw[0, i, :, at].astype(F32)
             ).astype(BF16)
         for r in range(2):
-            part = dot_t(xc[k, pl.ds(r * tall, tall)], xc[k])
+            part = dot_t(xc[k, pl.ds(r * tall, tall)], xc[k, pl.ds(r * tall, ff - r * tall)])
+            to = gram.at[pl.ds(r * tall, tall), pl.ds(r * tall, ff - r * tall)]
             if k:
-                part = gram[pl.ds(r * tall, tall)] + part
-            gram[pl.ds(r * tall, tall)] = part
+                part = to[...] + part
+            to[...] = part
             if k == chunks - 1:
-                g_out[r] = part.astype(BF16)
-                send(g_out.at[r], g_in.at[r], g_s.at[0, r], g_s.at[1, r], x=x, core=other)
+                blocks = [g_out.at[0], g_in.at[0]] if r == 0 else [ref.at[1, :, pl.ds(tall, tall)] for ref in (g_out, g_in)]
+                blocks[0][...] = part.astype(BF16)
+                send(blocks[0], blocks[1], g_s.at[0, r], g_s.at[1, r], x=x, core=other)
     norm = None
     diag = lax.broadcasted_iota(jnp.int32, (128, 128), 0) == lax.broadcasted_iota(jnp.int32, (128, 128), 1)
     for r in range(2):
-        arrived(g_in.at[r], g_s.at[1, r], g_s.at[0, r], x=x, core=other)
-        whole = gram[pl.ds(r * tall, tall)] + g_in[r].astype(F32)
-        gram[pl.ds(r * tall, tall)] = whole
+        came_in = g_in.at[r, :, pl.ds(r * tall, ff - r * tall)]
+        arrived(came_in, g_s.at[1, r], g_s.at[0, r], x=x, core=other)
+        to = gram.at[pl.ds(r * tall, tall), pl.ds(r * tall, ff - r * tall)]
+        whole = to[...] + came_in[...].astype(F32)
+        to[...] = whole
         for b in range(tall // 128):
-            square = whole[b * 128 : (b + 1) * 128, r * tall + b * 128 : r * tall + (b + 1) * 128]
+            square = whole[b * 128 : (b + 1) * 128, b * 128 : (b + 1) * 128]
             masked = jnp.where(diag, square, 0.0)
             norm = masked if norm is None else norm + masked
     norm = jnp.sum(jnp.sum(norm, axis=0, keepdims=True), axis=1, keepdims=True) + epsilon
     inverse = 1.0 / norm
     scale = (2.0 * half) ** 0.5 * lax.rsqrt(norm)
 
-    if STOP == 2:
-        out[0, :8, :128] = jnp.broadcast_to(inverse, (8, 128)).astype(BF16)
-        finish()
-        return
-    for r in range(2):
-        at = pl.ds(r * tall, tall)
-        n_ref[at] = (gram[at] * inverse).astype(BF16)
+    upper = (gram[:tall] * inverse).astype(BF16)
+    n_ref[:tall] = upper
+    n_ref[tall:, :tall] = upper[:, tall:].T
+    n_ref[tall:, tall:] = (gram[tall:, tall:] * inverse).astype(BF16)
     for r in range(2):
         at = pl.ds(r * tall, tall)
         eye = lax.broadcasted_iota(jnp.int32, (tall, ff), 0) + r * tall == lax.broadcasted_iota(jnp.int32, (tall, ff), 1)
@@ -391,10 +384,7 @@
         halfway = dot(p_ref[at], n_ref[...]).astype(BF16)
         c_ref[at] = dot_t(halfway, p_ref[...]).astype(BF16)
 
-    if STOP == 3:
-        out[0, :8, :128] = (c_ref[:8, :128].astype(F32) * scale).astype(BF16)
-        finish()
-        return
+
     pair = 2 * rows
 
     def cols(k):
@@ -413,31 +403,19 @@
             ubuf[i, 1, :, cols(k)] = u[rows:]
         if i == 0:
             for d in range(2):
-                send(ubuf.at[0, d], uhop.at[d], o_hop.at[0, d], o_hop.at[1, d], x=sides[d], core=c)
+                remote(ubuf.at[0, d], uhop.at[d], o_send, o_hop.at[d], x=sides[d], core=c).start()
         elif i < 3:
             d = i - 1
             for h in range(2):
-                send(
-                    ubuf.at[i, h], out.at[x, :, mine],
-                    o_d1.at[0, d, h], o_d1.at[1, d, c], x=sides[d], core=h,
-                )
+                remote(ubuf.at[i, h], out.at[x, :, mine], o_send, o_s, x=sides[d], core=h).start()
         else:
-            send(ubuf.at[3, other], out.at[x, :, mine], o_p.at[0], o_p.at[1], x=x, core=other)
-            stay = pltpu.make_async_copy(ubuf.at[3, c], out.at[x, :, mine], o_own)
-            stay.start()
+            send(ubuf.at[3, other], out.at[x, :, mine], o_mate, o_s, x=x, core=other)
+            pltpu.make_async_copy(ubuf.at[3, c], out.at[x, :, mine], o_s).start()
     for d in range(2):
-        arrived(uhop.at[d], o_hop.at[1, d], o_hop.at[0, d], x=sides[d], core=c)
-        send(uhop.at[d], out.at[came[d], :, mine], o_d2.at[0, d], o_d2.at[1, c], x=sides[d], core=d)
-    stay.wait()
-    arrived(out.at[x, :, theirs], o_p.at[1], o_p.at[0], x=x, core=other)
-    for d in range(2):
-        for h in range(2):
-            arrived(
-                out.at[came[d], :, pl.ds(h * half, half)], o_d1.at[1, d, h], o_d1.at[0, d, h],
-                x=sides[d], core=h,
-            )
-    for h in range(2):
-        arrived(out.at[x2, :, pl.ds(h * half, half)], o_d2.at[1, h], o_d2.at[0, h], x=xp, core=h)
+        arrived(uhop.at[d], o_hop.at[d], o_send, x=sides[d], core=c)
+        remote(uhop.at[d], out.at[came[d], :, mine], o_send, o_s, x=sides[d], core=d).start()
+    arrived(out, o_s, o_send, core=other)
+    gone(ubuf, o_send)
     finish()
 
 
@@ -483,25 +461,26 @@
             pltpu.VMEM((ff, ff), BF16),
             pltpu.VMEM((4, 2, rows, half), BF16),
             pltpu.VMEM((2, rows, half), BF16),
+            pltpu.VMEM((4 + sum(near) + 4, 1, 128), F32),
             pltpu.SemaphoreType.REGULAR,
             pltpu.SemaphoreType.REGULAR,
             dma((slots,)),
             dma,
-            dma((2, 8)),
-            dma((2, near[0])),
-            dma((2, near[1])),
+            dma,
+            dma,
+            dma,
+            dma,
+            dma,
+            dma,
+            dma,
+            dma,
+            dma,
+            dma((2,)),
+            dma,
+            dma,
             dma((2, 2)),
-            dma((2,)),
-            dma((2, 8)),
-            dma((2, 2, 2, 2)),
-            dma((2, 2, 2)),
-            dma((2, 2, 2)),
-            dma((2,)),
-            dma((2, 8)),
-            dma((2, 2)),
-            dma((2, 2)),
-            dma((2, 2)),
-            dma((2, 2, 2)),
+            dma,
+            dma,
             dma((2,)),
             dma,
         ],
@@ -509,7 +488,7 @@
             collective_id=0, has_side_effects=True, vmem_limit_bytes=55_200_000
         ),
         name="muon",
-    )(mom_values, mom_scale, gradients)
+    )(mom_values, pltpu.with_memory_space_constraint(mom_scale, pltpu.HBM), gradients)
 
 
 def solution(mesh):

time: 57.4 us -> 54.2 us (0.944)
  Pallas kernels: 55.6 us -> 53.1 us
  local copies, waits for them, and re-layouts: 1.65 us -> 0.97 us
    pallas_call x1, Pallas kernels: 55.6 us -> 53.1 us  [per_device(): pl.pallas_call(body, out_shape=jax.ShapeDtypeStruct(mom_values.shape, BF1...]
    unnamed x3 -> x1, local copies, waits for them, and re-layouts: 1.65 us -> 0.97 us
where the time goes in v4:
time: 54.2 us; the launch traced here: 54.1 us
  Pallas kernels  53.1 us (98%)
  local copies, waits for them, and re-layouts  0.97 us (2%)
    pallas_call x1, Pallas kernels, per_device(): pl.pallas_call(body, out_shape=jax.ShapeDtypeStruct(mom_values.shape, BF1...  53.1 us

profile of v4, /device:TPU:1, one launch (start us, length us, event | category | flops | bytes accessed | tf_op | source)
XLA Modules:
  0.0 54.1 jit_solution(8967468893927105611)
XLA Ops:
  0.0 53.1 %muon.1 = bf16[4,64,2048]{2,1,0:T(8,128)(2,1)S(1)} custom-call(bf16[4,64,2048]{2,1,0:T(8,128)(2,1)} %refs_0_.1, f32[4,64]{1,0:T(4,128)} %refs_1_.1, bf16[4,64,2048]{2,1,0:T(8,128)(2,1)} %refs_2_.1), custom_call_target="tpu_custom_call" | custom-call | tf_op jit(solution)/shard_map/muon/pallas_call | solution.py:434
  53.1 1.0 %copy.5 = bf16[4,64,2048]{2,1,0:T(8,128)(2,1)} copy(bf16[4,64,2048]{2,1,0:T(8,128)(2,1)S(1)} %muon.1) | data formatting | bytes 2097152

commit v5 on v4

--- a/solution.py
+++ b/solution.py
@@ -372,18 +372,13 @@
     n_ref[:tall] = upper
     n_ref[tall:, :tall] = upper[:, tall:].T
     n_ref[tall:, tall:] = (gram[tall:, tall:] * inverse).astype(BF16)
-    for r in range(2):
-        at = pl.ds(r * tall, tall)
-        eye = lax.broadcasted_iota(jnp.int32, (tall, ff), 0) + r * tall == lax.broadcasted_iota(jnp.int32, (tall, ff), 1)
-        square = dot(n_ref[at], n_ref[...])
-        p_ref[at] = (
-            jnp.where(eye, coeff_linear, 0.0) + coeff_cubic * n_ref[at].astype(F32) + coeff_quintic * square
-        ).astype(BF16)
-    for r in range(2):
-        at = pl.ds(r * tall, tall)
-        halfway = dot(p_ref[at], n_ref[...]).astype(BF16)
-        c_ref[at] = dot_t(halfway, p_ref[...]).astype(BF16)
-
+    eye = lax.broadcasted_iota(jnp.int32, (ff, ff), 0) == lax.broadcasted_iota(jnp.int32, (ff, ff), 1)
+    square = dot(n_ref[...], n_ref[...])
+    p_ref[...] = (
+        jnp.where(eye, coeff_linear, 0.0) + coeff_cubic * n_ref[...].astype(F32) + coeff_quintic * square
+    ).astype(BF16)
+    halfway = dot(p_ref[...], n_ref[...]).astype(BF16)
+    c_ref[...] = dot_t(halfway, p_ref[...]).astype(BF16)
 
     pair = 2 * rows
 

time: 54.2 us -> 54.1 us (level)
  no operation moved by 1% of the time
where the time goes in v5:
time: 54.1 us; the launch traced here: 53.9 us
  Pallas kernels  52.9 us (98%)
  local copies, waits for them, and re-layouts  0.97 us (2%)
    pallas_call x1, Pallas kernels, per_device(): pl.pallas_call(body, out_shape=jax.ShapeDtypeStruct(mom_values.shape, BF1...  52.9 us

profile of v5, /device:TPU:1, one launch (start us, length us, event | category | flops | bytes accessed | tf_op | source)
XLA Modules:
  0.0 53.9 jit_solution(16158484814305659534)
XLA Ops:
  0.0 52.9 %muon.1 = bf16[4,64,2048]{2,1,0:T(8,128)(2,1)S(1)} custom-call(bf16[4,64,2048]{2,1,0:T(8,128)(2,1)} %refs_0_.1, f32[4,64]{1,0:T(4,128)} %refs_1_.1, bf16[4,64,2048]{2,1,0:T(8,128)(2,1)} %refs_2_.1), custom_call_target="tpu_custom_call" | custom-call | tf_op jit(solution)/shard_map/muon/pallas_call | solution.py:429
  52.9 1.0 %copy.5 = bf16[4,64,2048]{2,1,0:T(8,128)(2,1)} copy(bf16[4,64,2048]{2,1,0:T(8,128)(2,1)S(1)} %muon.1) | data formatting | bytes 2097152
